TPU v7x, 256 devices: a whole 4x4x8 slice. The times are simulated.
256 devices in a mesh: ctx: 16 (over x, z_lo), sec: 8 (over y, core), dp: 2 (over z_hi).
Axes of the slice: x: 4, y: 4, z: 8 (z_hi: 2, z_lo: 4; z = z_hi * 4 + z_lo), core: 2. Of those that a mesh axis runs over, the one named last changes fastest.
Arguments:
- fresh_input: bfloat16 [2, 4096, 1536], P('dp', 'ctx'), may hold values from -6 to 6
- carried: bfloat16 [8, 2, 4096, 1536], P('sec', 'dp', 'ctx'), may hold values from -6 to 6
- qkv_weight: bfloat16 [8, 1536, 4608], P('sec', ('ctx', 'dp')), as said below
- out_weight: bfloat16 [8, 1536, 1536], P('sec', ('ctx', 'dp')), may hold values from -0.15625 to 0.15625
- rate_weight: bfloat16 [8, 1536, 6], P('sec', ('ctx', 'dp')), may hold values from -0.15625 to 0.15625
- fast_state: float32 [8, 2, 3, 6, 768, 256], P('sec', 'dp', None, None, 'ctx'), may hold values from -6 to 6
Outputs:
- passed: bfloat16 [8, 2, 4096, 1536], P('sec', 'dp', 'ctx')
- new_state: float32 [8, 2, 3, 6, 768, 256], P('sec', 'dp', None, None, 'ctx')
Inputs may be any that keep to these rules, and one draw needn't show every extreme that they name: Every entry of qkv_weight is at most 6 / sqrt(1536) in magnitude.
All inputs are finite; a program needn't handle non-finite values.
Results may differ from a plain program's by a relative error of at most 0.022.
Values may be sent and summed in bfloat16 or wider, within the bound.
No kernel may reach another device: no remote copies, remote signals or barrier semaphores. Data moves between devices by JAX's collectives and lax.ppermute only.
A program may use at most 128 MiB of HBM per device.

v0:
```python
import jax
import jax.numpy as jnp
from jax import lax
from jax.sharding import Mesh
from jax.sharding import PartitionSpec as P

CTX = ("xh", "xl", "zl")
CTX_DP = CTX + ("dp",)
LANES = 128
linear_coef = 3.4445
cubic_coef = -4.775
quintic_coef = 2.0315
update_scale = 8.0
highest = lax.Precision.HIGHEST


def swish(values):
    return values * jax.nn.sigmoid(values)


def unit_rows(values):
    return values / jnp.sqrt(jnp.sum(values * values, axis=-1, keepdims=True) + 1e-06)


def swap_pair(block):
    return lax.ppermute(block, "xh", [(0, 1), (1, 0)])


def pair_shard(low, high, is_low, dim):
    kept = jnp.where(is_low, low, high)
    got = swap_pair(jnp.where(is_low, high, low))
    return jnp.concatenate([jnp.where(is_low, kept, got), jnp.where(is_low, got, kept)], axis=dim)


def polynomial(square):
    return (
        linear_coef * jnp.eye(square.shape[-1], dtype=jnp.float32)
        + cubic_coef * square
        + quintic_coef * jnp.einsum("mde,mef->mdf", square, square, precision=highest)
    )


def orthogonalize(gradient):
    square = jnp.einsum("mrd,mre->mde", gradient, gradient, precision=highest)
    inverse_norm = lax.rsqrt(jnp.trace(square, axis1=-2, axis2=-1) + 1e-06)[:, None, None]
    square = square * inverse_norm * inverse_norm
    first = polynomial(square)
    square = jnp.einsum(
        "mde,mef->mdf",
        first,
        jnp.einsum("mde,mef->mdf", square, first, precision=highest),
        precision=highest,
    )
    both = jnp.einsum("mde,mef->mdf", first, polynomial(square), precision=highest)
    return jnp.einsum("mrd,mde->mre", gradient * inverse_norm, both, precision=highest)


def local(fresh_input, carried, qkv_weight, out_weight, rate_weight, fast_state):
    is_low = lax.axis_index("xh") == 0
    sections = lax.axis_size("sec")
    heads = rate_weight.shape[2]
    head_dim = fast_state.shape[5]
    half = heads // 2
    width = half * head_dim
    rows = qkv_weight.shape[1]
    count, channels = fresh_input.shape[1:]
    w = qkv_weight[0].reshape(rows, 3, 2, width)
    rates = jnp.pad(rate_weight[0].reshape(rows, 2, half), ((0, 0), (0, 0), (0, LANES - half)))
    low, high = (
        jnp.concatenate([w[:, 0, h], w[:, 1, h], w[:, 2, h], rates[:, h]], axis=1) for h in (0, 1)
    )
    group_w = lax.all_gather(
        pair_shard(low, high, is_low, 0), ("xl", "zl", "dp"), axis=0, tiled=True
    )
    previous = fast_state[0, 0]
    shard = previous.astype(jnp.bfloat16)
    group_fast = lax.all_gather(
        pair_shard(shard[:, :half], shard[:, half:], is_low, 2), ("xl", "zl"), axis=2, tiled=True
    )
    group_out = lax.all_gather(out_weight[0], ("xl", "zl", "dp"), axis=0, tiled=True)
    is_last = lax.axis_index("sec") == sections - 1
    source = jnp.where(is_last, fresh_input[0], carried[0, 0])
    mine = lax.ppermute(source, "sec", [(i, (i + 1) % sections) for i in range(sections)])
    pairs = [
        (a * sections + i, (1 - a) * sections + (i + 1) % sections)
        for a in (0, 1)
        for i in range(sections)
    ]
    other = lax.ppermute(source, ("xh", "sec"), pairs)
    inputs = jnp.concatenate([mine, other], axis=0)
    ordered = (
        inputs.reshape(2 * count, 2, -1, rows).transpose(0, 2, 1, 3).reshape(2 * count, channels)
    )
    projected = jnp.dot(ordered, group_w, preferred_element_type=jnp.float32)
    part = lambda i: projected[:, i * width : (i + 1) * width].reshape(2 * count, half, head_dim)
    query_rows = unit_rows(swish(part(0))).astype(jnp.bfloat16)
    key_rows = unit_rows(swish(part(1))).astype(jnp.bfloat16)
    value_rows = part(2).astype(jnp.bfloat16)
    rates = jax.nn.softplus(projected[:, 3 * width : 3 * width + half])
    gate_fast, up_fast, down_fast = (group_fast[0], group_fast[1], group_fast[2])
    gate_pre = jnp.einsum("thd,hfd->htf", key_rows, gate_fast, preferred_element_type=jnp.float32)
    up_pre = jnp.einsum("thd,hfd->htf", key_rows, up_fast, preferred_element_type=jnp.float32)
    sigma = jax.nn.sigmoid(gate_pre)
    gate_act = gate_pre * sigma
    key_hidden = (gate_act * up_pre).astype(jnp.bfloat16)
    scaled_values = (rates[:, :, None] * value_rows.astype(jnp.float32)).astype(jnp.bfloat16)
    hidden_grad = -jnp.einsum(
        "thd,hfd->htf", scaled_values, down_fast, preferred_element_type=jnp.float32
    )
    up_grad = (hidden_grad * gate_act).astype(jnp.bfloat16)
    gate_grad = (hidden_grad * up_pre * sigma * (1.0 + gate_pre * (1.0 - sigma))).astype(
        jnp.bfloat16
    )
    grad_gate = jnp.einsum("htf,thd->hfd", gate_grad, key_rows, preferred_element_type=jnp.float32)
    grad_up = jnp.einsum("htf,thd->hfd", up_grad, key_rows, preferred_element_type=jnp.float32)
    grad_down = -jnp.einsum(
        "htf,thd->hfd", key_hidden, scaled_values, preferred_element_type=jnp.float32
    )
    owners = lax.axis_size(("xl", "zl"))
    spread = jnp.concatenate([grad_gate, grad_up, grad_down[: owners - 2 * half]], axis=0)
    shared = lax.psum(grad_down[owners - 2 * half :].astype(jnp.bfloat16), ("xl", "zl"))
    owned = lax.psum_scatter(
        spread.astype(jnp.bfloat16), ("xl", "zl"), scatter_dimension=0, tiled=True
    )
    gradient = jnp.concatenate([owned, shared], axis=0).astype(jnp.float32)
    current = orthogonalize(gradient).astype(jnp.bfloat16)
    shard_rows = previous.shape[2]
    blocks = current.reshape(2, owners, 2, shard_rows, head_dim)
    outgoing = blocks[0].transpose(1, 0, 2, 3).reshape(2 * owners, shard_rows, head_dim)
    arrived = lax.all_to_all(outgoing, CTX, 0, 0, tiled=True)
    arrived = arrived.reshape(2, owners, shard_rows, head_dim)
    mine_last = lax.dynamic_index_in_dim(blocks[1], lax.axis_index(("xl", "zl")), 0, keepdims=False)
    last = pair_shard(mine_last[0][None], mine_last[1][None], is_low, 0)[:, None]
    current = jnp.concatenate([arrived, last], axis=1).astype(jnp.float32)
    current = current.reshape(2, 3, half, shard_rows, head_dim).transpose(1, 0, 2, 3, 4)
    current = current.reshape(previous.shape)
    stepped = previous - update_scale * current
    rescale = jnp.sqrt(jnp.mean(previous * previous, axis=-1, keepdims=True) + 1e-06) * lax.rsqrt(
        jnp.mean(stepped * stepped, axis=-1, keepdims=True) + 1e-06
    )
    new_state = (stepped * rescale)[None, None]
    gate_query = jnp.einsum(
        "thd,hfd->htf", query_rows, gate_fast, preferred_element_type=jnp.float32
    )
    up_query = jnp.einsum("thd,hfd->htf", query_rows, up_fast, preferred_element_type=jnp.float32)
    hidden = (swish(gate_query) * up_query).astype(jnp.bfloat16)
    mixture = jnp.einsum("htf,hfd->thd", hidden, down_fast, preferred_element_type=jnp.float32)
    head_out = (
        mixture * lax.rsqrt(jnp.mean(mixture * mixture, axis=-1, keepdims=True) + 1e-05)
    ).astype(jnp.bfloat16)
    branch_out = jnp.dot(
        head_out.reshape(2 * count, width), group_out, preferred_element_type=jnp.float32
    )
    from_pair = swap_pair(branch_out[count:].astype(jnp.bfloat16))
    passed = (
        mine.astype(jnp.float32) + (branch_out[:count] + from_pair.astype(jnp.float32))
    ).astype(jnp.bfloat16)
    return (passed[None, None], new_state)


def solution(mesh):
    shape = (2, 2, 4, mesh.shape["sec"], mesh.shape["dp"])
    split = Mesh(mesh.devices.reshape(shape), ("xh", "xl", "zl", "sec", "dp"))
    in_specs = (
        P("dp", CTX, None),
        P("sec", "dp", CTX, None),
        P("sec", CTX_DP, None),
        P("sec", CTX_DP, None),
        P("sec", CTX_DP, None),
        P("sec", "dp", None, None, CTX, None),
    )
    out_specs = (P("sec", "dp", CTX, None), P("sec", "dp", None, None, CTX, None))
    return jax.shard_map(local, mesh=split, in_specs=in_specs, out_specs=out_specs, check_vma=False)
```

profile of v0, /device:TPU:8, one launch (start us, length us, event | category | flops | bytes accessed | tf_op | source)
XLA Modules:
  0.0 848.2 jit_solution(16667933280861583742)
XLA Ops:
  10.0 3.1 collective-permute-start.3
  13.1 5.9 collective-permute-done.3
  20.1 3.1 collective-permute-start.1
  23.2 4.8 collective-permute-done.1
  29.9 3.4 collective-permute-start
  33.4 19.9 %collective-permute-done.2 = bf16[256,1536]{1,0:T(8,128)(2,1)S(1)} collective-permute-done((bf16[256,1536]{1,0:T(8,128)(2,1)S(1)}, bf16[256,1536]{1,0:T(8,128)(2,1)S(1)}, u32[]{:S(2)}, u32[]{:S(2)}) %collective-permute-start.2) | collective-permute-done | bytes 786464 | tf_op jit(solution)/shard_map/ppermute | solution.py:89
  55.2 358.9 %all-gather.7.cloned.1.call-done = bf16[1536,2432]{1,0:T(8,128)(2,1)} async-done(((bf16[96,2432]{1,0:T(8,128)(2,1)}), bf16[1536,2432]{1,0:T(8,128)(2,1)}) %all-gather.7.cloned.1.call-update) | async-done | bytes 7471120 | tf_op jit(solution)/shard_map/all_gather | solution.py:72
  414.1 6.8 fusion.47
  420.9 1.9 fusion.44
  427.3 71.4 %all-gather.5.cloned.1.call-done = bf16[3,3,768,256]{3,2,1,0:T(8,128)(2,1)} async-done(((bf16[3,3,96,256]{3,2,1,0:T(8,128)(2,1)}), bf16[3,3,768,256]{3,2,1,0:T(8,128)(2,1)}) %all-gather.5.cloned.1.call-update) | async-done | bytes 3538960 | tf_op jit(solution)/shard_map/all_gather | solution.py:77
  498.6 2.5 fusion.26
  505.4 4.6 fusion.17
  510.0 5.3 fusion.16
  520.2 4.5 fusion.25
  524.7 5.7 fusion.11
  531.5 115.1 %all-gather.9.cloned.1.call-done = bf16[1,768,1536]{2,1,0:T(8,128)(2,1)} async-done(((bf16[1,48,1536]{2,1,0:T(8,128)(2,1)}), bf16[1,768,1536]{2,1,0:T(8,128)(2,1)}) %all-gather.9.cloned.1.call-update) | async-done | bytes 2359312 | tf_op jit(solution)/shard_map/all_gather | solution.py:80
  646.5 3.3 fusion.3
  650.8 75.1 %reduce-scatter.2.cloned.1.call-done = bf16[1,768,256]{2,1,0:T(8,128)(2,1)} async-done(((bf16[8,768,256]{2,1,0:T(8,128)(2,1)}), bf16[1,768,256]{2,1,0:T(8,128)(2,1)}) %reduce-scatter.2.cloned.1.call-update) | async-done | bytes 393232 | tf_op jit(solution)/shard_map/reduce_scatter | solution.py:122
  727.7 84.6 %all-reduce.3.cloned.1.call-done = bf16[1,768,256]{2,1,0:T(8,128)(2,1)} async-done(((bf16[1,768,256]{2,1,0:T(8,128)(2,1)}), bf16[1,768,256]{2,1,0:T(8,128)(2,1)}) %all-reduce.3.cloned.1.call-update) | async-done | bytes 393232 | tf_op jit(solution)/shard_map/psum | solution.py:121
  814.1 1.9 select_reduce_fusion
  822.0 2.7 collective-permute-start.5
  825.5 3.6 all-to-all-start
  829.1 2.5 fusion.32
  832.4 7.5 all-to-all-done
  (101 shorter events, 35.8 us)
Async XLA Ops:
  7.2 407.0 %all-gather.7.cloned.1.call-start = ((), (), s32[]{:S(2)}) async-start(), calls=%async_computation.3 | async-start | bytes 7938048 | tf_op jit(solution)/shard_map/all_gather | solution.py:72
  9.9 10.1 %copy-start.1 = (f32[1,1,3,6,48,256]{5,4,3,2,1,0:T(8,128)S(1)}, f32[1,1,3,6,48,256]{5,4,3,2,1,0:T(8,128)}, u32[]{:S(2)}) copy-start(f32[1,1,3,6,48,256]{5,4,3,2,1,0:T(8,128)} %param.11) | copy-start | bytes 2654212
  10.0 9.0 %collective-permute-start.3 = (bf16[48,2432]{1,0:T(8,128)(2,1)S(1)}, bf16[48,2432]{1,0:T(8,128)(2,1)S(1)}, u32[]{:S(2)}, u32[]{:S(2)}) collective-permute-start(bf16[48,2432]{1,0:T(8,128)(2,1)S(1)} %broadcast_select_fusion.2), channel_id=1, source_target_pairs={{0,128},{128,0},{1,129},{129,1},{2,130},{130,2},{3,131},{131,3},{4... | collective-permute-start | bytes 700424 | tf_op jit(solution)/shard_map/ppermute | solution.py:26
  19.9 478.7 %all-gather.5.cloned.1.call-start = ((), (), s32[]{:S(2)}) async-start(), calls=%async_computation.2 | async-start | bytes 3981312 | tf_op jit(solution)/shard_map/all_gather | solution.py:77
  20.0 9.0 %copy-start.8 = (bf16[1,1,256,1536]{3,2,1,0:T(8,128)(2,1)S(1)}, bf16[1,1,256,1536]{3,2,1,0:T(8,128)(2,1)}, u32[]{:S(2)}) copy-start(bf16[1,1,256,1536]{3,2,1,0:T(8,128)(2,1)} %param.7) | copy-start | bytes 2359300
  20.1 9.0 %copy-start.9 = (bf16[1,256,1536]{2,1,0:T(8,128)(2,1)S(1)}, bf16[1,256,1536]{2,1,0:T(8,128)(2,1)}, u32[]{:S(2)}) copy-start(bf16[1,256,1536]{2,1,0:T(8,128)(2,1)} %param.6) | copy-start | bytes 2359300
  20.1 7.9 collective-permute-start.1
  28.9 617.6 %all-gather.9.cloned.1.call-start = ((), (), s32[]{:S(2)}) async-start(), calls=%async_computation.6 | async-start | bytes 2506752 | tf_op jit(solution)/shard_map/all_gather | solution.py:80
  29.1 24.2 %collective-permute-start.2 = (bf16[256,1536]{1,0:T(8,128)(2,1)S(1)}, bf16[256,1536]{1,0:T(8,128)(2,1)S(1)}, u32[]{:S(2)}, u32[]{:S(2)}) collective-permute-start(bf16[256,1536]{1,0:T(8,128)(2,1)S(1)} %bitcast_select_fusion), channel_id=1, source_target_pairs={{0,130},{2,132},{4,134},{6,136},{8,138},{10,140},{12,142},{14,128}... | collective-permute-start | bytes 2359304 | tf_op jit(solution)/shard_map/ppermute | solution.py:89
  29.9 23.4 %collective-permute-start = (bf16[256,1536]{1,0:T(8,128)(2,1)S(1)}, bf16[256,1536]{1,0:T(8,128)(2,1)S(1)}, u32[]{:S(2)}, u32[]{:S(2)}) collective-permute-start(bf16[256,1536]{1,0:T(8,128)(2,1)S(1)} %bitcast_select_fusion), channel_id=1, source_target_pairs={{0,2},{2,4},{4,6},{6,8},{8,10},{10,12},{12,14},{14,0},{1,3},{3,5},... | collective-permute-start | bytes 2359304 | tf_op jit(solution)/shard_map/ppermute | solution.py:83
  33.4 692.6 %reduce-scatter.2.cloned.1.call-start = ((), (), s32[]{:S(2)}) async-start(), calls=%async_computation.4 | async-start | bytes 3538944 | tf_op jit(solution)/shard_map/reduce_scatter | solution.py:122
  498.6 2.5 copy-start.11
  501.1 1.4 copy-start.4
  502.2 2.2 copy-start.12
  510.0 5.3 slice-start
  517.2 1.3 copy-start.6
  517.2 2.1 copy-start.3
  517.2 295.1 %all-reduce.3.cloned.1.call-start = ((), (), s32[]{:S(2)}) async-start(), calls=%async_computation.5 | async-start | bytes 786432 | tf_op jit(solution)/shard_map/psum | solution.py:121
  650.8 178.3 %collective-permute-start.4 = (bf16[256,1536]{1,0:T(8,128)(2,1)}, bf16[256,1536]{1,0:T(8,128)(2,1)}, u32[]{:S(2)}, u32[]{:S(2)}) collective-permute-start(bf16[256,1536]{1,0:T(8,128)(2,1)} %slice.169), channel_id=1, source_target_pairs={{0,128},{128,0},{1,129},{129,1},{2,130},{130,2},{3,131},{131,3},{4... | collective-permute-start | bytes 2359304 | tf_op jit(solution)/shard_map/ppermute | solution.py:26
  818.3 1.4 copy-start
  821.3 4.2 copy-start.10
  822.0 9.6 %collective-permute-start.5 = (bf16[1,48,256]{2,1,0:T(8,128)(2,1)}, bf16[1,48,256]{2,1,0:T(8,128)(2,1)}, u32[]{:S(2)}, u32[]{:S(2)}) collective-permute-start(bf16[1,48,256]{2,1,0:T(8,128)(2,1)} %select_bitcast_fusion), channel_id=1, source_target_pairs={{0,128},{128,0},{1,129},{129,1},{2,130},{130,2},{3,131},{131,3},{4... | collective-permute-start | bytes 73736 | tf_op jit(solution)/shard_map/ppermute | solution.py:26
  825.5 14.4 %all-to-all-start = ((bf16[16,48,256]{2,1,0:T(8,128)(2,1)}), bf16[16,48,256]{2,1,0:T(8,128)(2,1)S(1)}, u32[]{:S(2)}, u32[]{:S(2)}) async-start(bf16[16,48,256]{2,1,0:T(8,128)(2,1)} %bitcast.20), calls=%async_computation.1 | async-start | bytes 786432 | tf_op jit(solution)/shard_map/all_to_all | solution.py:130
  832.4 7.7 copy-start.2
  (2 other events, 1.9 us)
Sparse Core Ops, SparseCore 0:
  20.0 394.0 all-gather.6
  415.9 82.6 all-gather.4
  500.4 146.0 all-gather.8
  648.9 76.9 reduce-scatter.1
  728.4 83.8 all-reduce.2
where the time goes:
time: 849 us; the launch traced here: 848 us
  waiting for transfers between devices  743 us (88%)
  matrix products  43.5 us (5%)
  local copies, waits for them, and re-layouts  17.9 us (2%)
  starting transfers between devices  17.1 us (2%)
  between operations  14.3 us (2%)
  other arithmetic  12 us (1%)
    all_gather x1, waiting for transfers between devices, local(): lax.all_gather(pair_shard(low, high, is_low, 0), ('xl', 'zl', 'dp'), axis...  359 us
    all_gather x1, waiting for transfers between devices, local(): lax.all_gather(out_weight[0], ('xl', 'zl', 'dp'), axis=0, tiled=True)  115 us
    psum x1, waiting for transfers between devices, local(): lax.psum(grad_down[owners - 2 * half:].astype(jnp.bfloat16), ('xl', 'zl'))  84.6 us
    reduce_scatter x1, waiting for transfers between devices, local(): lax.psum_scatter(spread.astype(jnp.bfloat16), ('xl', 'zl'), scatter_dimen...  75.1 us
    all_gather x1, waiting for transfers between devices, local(): lax.all_gather(pair_shard(shard[:, :half], shard[:, half:], is_low, 2), (...  71.4 us
    ppermute x1, waiting for transfers between devices, local(): other = lax.ppermute(source, ('xh', 'sec'), pairs)  19.9 us
  transfers between devices with their start and end apart: 12, of which 9 were waited for; matrix products, arithmetic and copies ran while one was open for 8% of the time, Pallas kernels for 0%

commit v1 on v0

--- a/solution.py
+++ b/solution.py
@@ -1,8 +1,10 @@
+import functools
 import jax
 import jax.numpy as jnp
 from jax import lax
 from jax.sharding import Mesh
 from jax.sharding import PartitionSpec as P
+from jax.lax import all_to_all, axis_size
 
 CTX = ("xh", "xl", "zl")
 CTX_DP = CTX + ("dp",)
@@ -12,6 +14,19 @@
 quintic_coef = 2.0315
 update_scale = 8.0
 highest = lax.Precision.HIGHEST
+
+
+def lift_the_patch(field, device_axis, dimension_no):
+    local_now = jnp.concatenate(
+        all_to_all(jnp.stack([field] * axis_size(device_axis), axis=0), device_axis, 0, 0),
+        dimension_no,
+    )
+    return local_now
+
+
+shape_the_regions = functools.partial(
+    lift_the_patch, device_axis=("xl", "zl", "dp"), dimension_no=0
+)
 
 
 def swish(values):
@@ -69,9 +84,7 @@
     low, high = (
         jnp.concatenate([w[:, 0, h], w[:, 1, h], w[:, 2, h], rates[:, h]], axis=1) for h in (0, 1)
     )
-    group_w = lax.all_gather(
-        pair_shard(low, high, is_low, 0), ("xl", "zl", "dp"), axis=0, tiled=True
-    )
+    group_w = shape_the_regions(pair_shard(low, high, is_low, 0))
     previous = fast_state[0, 0]
     shard = previous.astype(jnp.bfloat16)
     group_fast = lax.all_gather(

time: 849 us -> 631 us (0.74)
  waiting for transfers between devices: 743 us -> 512 us
  starting transfers between devices: 17.1 us -> 27.3 us
    all_gather x1 -> x0, waiting for transfers between devices: 359 us -> none  [local(): lax.all_gather(pair_shard(low, high, is_low, 0), ('xl', 'zl', 'dp'), axis...]
    all_to_all x0 -> x1, waiting for transfers between devices: none -> 157 us  [lift_the_patch(): all_to_all(jnp.stack([field] * axis_size(device_axis), axis=0), device_ax...]
    all_gather x1, waiting for transfers between devices: 71.4 us -> 0.01 us  [local(): lax.all_gather(pair_shard(shard[:, :half], shard[:, half:], is_low, 2), (...]
    ppermute x4, waiting for transfers between devices: 10.7 us -> 60 us  [swap_pair(): return lax.ppermute(block, 'xh', [(0, 1), (1, 0)])]
    all_to_all x0 -> x1, starting transfers between devices: none -> 9.67 us  [lift_the_patch(): all_to_all(jnp.stack([field] * axis_size(device_axis), axis=0), device_ax...]
  transfers between devices with their start and end apart: 12 -> 12, of which waited for: 9 -> 8; matrix products, arithmetic and copies ran while one was open for 8% -> 10% of each run, Pallas kernels for 0% -> 0%
where the time goes in v1:
time: 631 us; the launch traced here: 630 us
  waiting for transfers between devices  512 us (81%)
  matrix products  43.5 us (7%)
  starting transfers between devices  27.3 us (4%)
  local copies, waits for them, and re-layouts  21.7 us (3%)
  between operations  14.3 us (2%)
  other arithmetic  11.1 us (2%)
    all_to_all x1, waiting for transfers between devices, lift_the_patch(): all_to_all(jnp.stack([field] * axis_size(device_axis), axis=0), device_ax...  157 us
    all_gather x1, waiting for transfers between devices, local(): lax.all_gather(out_weight[0], ('xl', 'zl', 'dp'), axis=0, tiled=True)  113 us
    psum x1, waiting for transfers between devices, local(): lax.psum(grad_down[owners - 2 * half:].astype(jnp.bfloat16), ('xl', 'zl'))  84.6 us
    reduce_scatter x1, waiting for transfers between devices, local(): lax.psum_scatter(spread.astype(jnp.bfloat16), ('xl', 'zl'), scatter_dimen...  71.9 us
    ppermute x4, waiting for transfers between devices, swap_pair(): return lax.ppermute(block, 'xh', [(0, 1), (1, 0)])  60 us
    ppermute x1, waiting for transfers between devices, local(): other = lax.ppermute(source, ('xh', 'sec'), pairs)  18.9 us
  transfers between devices with their start and end apart: 12, of which 8 were waited for; matrix products, arithmetic and copies ran while one was open for 10% of the time, Pallas kernels for 0%

profile of v1, /device:TPU:8, one launch (start us, length us, event | category | flops | bytes accessed | tf_op | source)
XLA Modules:
  0.0 630.4 jit_solution(9816814272714296542)
XLA Ops:
  9.9 3.1 collective-permute-start.3
  13.0 5.9 collective-permute-done.3
  19.1 3.6 stack.2
  22.6 9.7 %all-to-all-start = ((bf16[16,96,2432]{2,1,0:T(8,128)(2,1)}), bf16[16,96,2432]{2,1,0:T(8,128)(2,1)}, u32[]{:S(2)}, u32[]{:S(2)}) async-start(bf16[16,96,2432]{2,1,0:T(8,128)(2,1)} %stack.2), calls=%async_computation | async-start | bytes 14942208 | tf_op jit(solution)/shard_map/all_to_all | solution.py:21
  32.5 2.8 collective-permute-start.1
  35.3 54.1 %collective-permute-done.1 = bf16[3,3,48,256]{3,2,1,0:T(8,128)(2,1)S(1)} collective-permute-done((bf16[3,3,48,256]{3,2,1,0:T(8,128)(2,1)S(1)}, bf16[3,3,48,256]{3,2,1,0:T(8,128)(2,1)S(1)}, u32[]{:S(2)}, u32[]{:S(2)}) %collective-permute-start.1) | collective-permute-done | bytes 221216 | tf_op jit(solution)/shard_map/ppermute | solution.py:41
  92.6 18.9 %collective-permute-done.2 = bf16[256,1536]{1,0:T(8,128)(2,1)S(1)} collective-permute-done((bf16[256,1536]{1,0:T(8,128)(2,1)S(1)}, bf16[256,1536]{1,0:T(8,128)(2,1)S(1)}, u32[]{:S(2)}, u32[]{:S(2)}) %collective-permute-start.2) | collective-permute-done | bytes 786464 | tf_op jit(solution)/shard_map/ppermute | solution.py:102
  113.3 156.9 %all-to-all-done = bf16[16,96,2432]{2,1,0:T(8,128)(2,1)} async-done(((bf16[16,96,2432]{2,1,0:T(8,128)(2,1)}), bf16[16,96,2432]{2,1,0:T(8,128)(2,1)}, u32[]{:S(2)}, u32[]{:S(2)}) %all-to-all-start) | async-done | bytes 7471136 | tf_op jit(solution)/shard_map/all_to_all | solution.py:21
  270.1 6.9 %fusion.47 = f32[512,2432]{1,0:T(8,128)S(1)} fusion(bf16[512,1536]{0,1:T(8,128)(2,1)S(1)} %bitcast.116, bf16[1536,2432]{1,0:T(8,128)(2,1)} %bitcast.9), kind=kOutput, calls=%fused_computation.110 | convolution fusion | flops 3825205248 | bytes 14024704 | tf_op jit(solution)/shard_map/dot_general | solution.py:107
  277.0 2.0 fusion.44
  283.5 2.5 fusion.26
  290.3 4.6 fusion.17
  294.9 5.3 fusion.16
  305.0 4.5 fusion.25
  309.5 5.6 fusion.11
  316.3 112.6 %all-gather.6.cloned.1.call-done = bf16[1,768,1536]{2,1,0:T(8,128)(2,1)} async-done(((bf16[1,48,1536]{2,1,0:T(8,128)(2,1)}), bf16[1,768,1536]{2,1,0:T(8,128)(2,1)}) %all-gather.6.cloned.1.call-update) | async-done | bytes 2359312 | tf_op jit(solution)/shard_map/all_gather | solution.py:93
  428.9 3.3 fusion.3
  433.2 3.0 collective-permute-start.4
  436.3 71.9 %reduce-scatter.2.cloned.1.call-done = bf16[1,768,256]{2,1,0:T(8,128)(2,1)} async-done(((bf16[8,768,256]{2,1,0:T(8,128)(2,1)}), bf16[1,768,256]{2,1,0:T(8,128)(2,1)}) %reduce-scatter.2.cloned.1.call-update) | async-done | bytes 393232 | tf_op jit(solution)/shard_map/reduce_scatter | solution.py:135
  509.9 84.6 %all-reduce.3.cloned.1.call-done = bf16[1,768,256]{2,1,0:T(8,128)(2,1)} async-done(((bf16[1,768,256]{2,1,0:T(8,128)(2,1)}), bf16[1,768,256]{2,1,0:T(8,128)(2,1)}) %all-reduce.3.cloned.1.call-update) | async-done | bytes 393232 | tf_op jit(solution)/shard_map/psum | solution.py:134
  604.2 2.7 collective-permute-start.5
  607.7 3.6 all-to-all-start.1
  611.3 2.5 fusion.32
  614.7 7.5 %all-to-all-done.1 = bf16[16,48,256]{2,1,0:T(8,128)(2,1)S(1)} async-done(((bf16[16,48,256]{2,1,0:T(8,128)(2,1)}), bf16[16,48,256]{2,1,0:T(8,128)(2,1)S(1)}, u32[]{:S(2)}, u32[]{:S(2)}) %all-to-all-start.1) | async-done | bytes 393248 | tf_op jit(solution)/shard_map/all_to_all | solution.py:143
  (101 shorter events, 38.1 us)
Async XLA Ops:
  9.9 9.0 %collective-permute-start.3 = (bf16[48,2432]{1,0:T(8,128)(2,1)S(1)}, bf16[48,2432]{1,0:T(8,128)(2,1)S(1)}, u32[]{:S(2)}, u32[]{:S(2)}) collective-permute-start(bf16[48,2432]{1,0:T(8,128)(2,1)S(1)} %broadcast_select_fusion.2), channel_id=1, source_target_pairs={{0,128},{128,0},{1,129},{129,1},{2,130},{130,2},{3,131},{131,3},{4... | collective-permute-start | bytes 700424 | tf_op jit(solution)/shard_map/ppermute | solution.py:41
  22.6 9.7 %copy-start.1 = (f32[1,1,3,6,48,256]{5,4,3,2,1,0:T(8,128)S(1)}, f32[1,1,3,6,48,256]{5,4,3,2,1,0:T(8,128)}, u32[]{:S(2)}) copy-start(f32[1,1,3,6,48,256]{5,4,3,2,1,0:T(8,128)} %param.11) | copy-start | bytes 2654212
  22.6 247.5 %all-to-all-start = ((bf16[16,96,2432]{2,1,0:T(8,128)(2,1)}), bf16[16,96,2432]{2,1,0:T(8,128)(2,1)}, u32[]{:S(2)}, u32[]{:S(2)}) async-start(bf16[16,96,2432]{2,1,0:T(8,128)(2,1)} %stack.2), calls=%async_computation | async-start | bytes 14942208 | tf_op jit(solution)/shard_map/all_to_all | solution.py:21
  32.3 251.1 %all-gather.4.cloned.1.call-start = ((), (), s32[]{:S(2)}) async-start(), calls=%async_computation.3 | async-start | bytes 3981312 | tf_op jit(solution)/shard_map/all_gather | solution.py:90
  32.4 57.9 %copy-start.8 = (bf16[1,1,256,1536]{3,2,1,0:T(8,128)(2,1)S(1)}, bf16[1,1,256,1536]{3,2,1,0:T(8,128)(2,1)}, u32[]{:S(2)}) copy-start(bf16[1,1,256,1536]{3,2,1,0:T(8,128)(2,1)} %param.7) | copy-start | bytes 2359300
  32.4 57.9 %copy-start.9 = (bf16[1,256,1536]{2,1,0:T(8,128)(2,1)S(1)}, bf16[1,256,1536]{2,1,0:T(8,128)(2,1)}, u32[]{:S(2)}) copy-start(bf16[1,256,1536]{2,1,0:T(8,128)(2,1)} %param.6) | copy-start | bytes 2359300
  32.5 56.9 %collective-permute-start.1 = (bf16[3,3,48,256]{3,2,1,0:T(8,128)(2,1)S(1)}, bf16[3,3,48,256]{3,2,1,0:T(8,128)(2,1)S(1)}, u32[]{:S(2)}, u32[]{:S(2)}) collective-permute-start(bf16[3,3,48,256]{3,2,1,0:T(8,128)(2,1)S(1)} %broadcast_select_fusion.6), channel_id=1, source_target_pairs={{0,128},{128,0},{1,129},{129,1},{2,130},{130,2},{3,131},{131,3},{4... | collective-permute-start | bytes 663560 | tf_op jit(solution)/shard_map/ppermute | solution.py:41
  90.3 338.6 %all-gather.6.cloned.1.call-start = ((), (), s32[]{:S(2)}) async-start(), calls=%async_computation.6 | async-start | bytes 2506752 | tf_op jit(solution)/shard_map/all_gather | solution.py:93
  90.5 20.9 %collective-permute-start.2 = (bf16[256,1536]{1,0:T(8,128)(2,1)S(1)}, bf16[256,1536]{1,0:T(8,128)(2,1)S(1)}, u32[]{:S(2)}, u32[]{:S(2)}) collective-permute-start(bf16[256,1536]{1,0:T(8,128)(2,1)S(1)} %bitcast_select_fusion), channel_id=1, source_target_pairs={{0,130},{2,132},{4,134},{6,136},{8,138},{10,140},{12,142},{14,128}... | collective-permute-start | bytes 2359304 | tf_op jit(solution)/shard_map/ppermute | solution.py:102
  90.6 20.8 %collective-permute-start = (bf16[256,1536]{1,0:T(8,128)(2,1)S(1)}, bf16[256,1536]{1,0:T(8,128)(2,1)S(1)}, u32[]{:S(2)}, u32[]{:S(2)}) collective-permute-start(bf16[256,1536]{1,0:T(8,128)(2,1)S(1)} %bitcast_select_fusion), channel_id=1, source_target_pairs={{0,2},{2,4},{4,6},{6,8},{8,10},{10,12},{12,14},{14,0},{1,3},{3,5},... | collective-permute-start | bytes 2359304 | tf_op jit(solution)/shard_map/ppermute | solution.py:96
  92.5 415.6 %reduce-scatter.2.cloned.1.call-start = ((), (), s32[]{:S(2)}) async-start(), calls=%async_computation.4 | async-start | bytes 3538944 | tf_op jit(solution)/shard_map/reduce_scatter | solution.py:135
  283.4 2.5 copy-start.11
  286.0 1.4 copy-start.4
  287.0 2.2 copy-start.12
  294.9 5.3 slice-start
  302.0 1.3 copy-start.6
  302.0 2.1 copy-start.3
  302.0 292.5 %all-reduce.3.cloned.1.call-start = ((), (), s32[]{:S(2)}) async-start(), calls=%async_computation.5 | async-start | bytes 786432 | tf_op jit(solution)/shard_map/psum | solution.py:134
  433.2 178.1 %collective-permute-start.4 = (bf16[256,1536]{1,0:T(8,128)(2,1)}, bf16[256,1536]{1,0:T(8,128)(2,1)}, u32[]{:S(2)}, u32[]{:S(2)}) collective-permute-start(bf16[256,1536]{1,0:T(8,128)(2,1)} %slice.169), channel_id=1, source_target_pairs={{0,128},{128,0},{1,129},{129,1},{2,130},{130,2},{3,131},{131,3},{4... | collective-permute-start | bytes 2359304 | tf_op jit(solution)/shard_map/ppermute | solution.py:41
  600.4 1.4 copy-start
  603.5 4.2 copy-start.10
  604.2 9.6 %collective-permute-start.5 = (bf16[1,48,256]{2,1,0:T(8,128)(2,1)}, bf16[1,48,256]{2,1,0:T(8,128)(2,1)}, u32[]{:S(2)}, u32[]{:S(2)}) collective-permute-start(bf16[1,48,256]{2,1,0:T(8,128)(2,1)} %select_bitcast_fusion), channel_id=1, source_target_pairs={{0,128},{128,0},{1,129},{129,1},{2,130},{130,2},{3,131},{131,3},{4... | collective-permute-start | bytes 73736 | tf_op jit(solution)/shard_map/ppermute | solution.py:41
  607.7 14.4 %all-to-all-start.1 = ((bf16[16,48,256]{2,1,0:T(8,128)(2,1)}), bf16[16,48,256]{2,1,0:T(8,128)(2,1)S(1)}, u32[]{:S(2)}, u32[]{:S(2)}) async-start(bf16[16,48,256]{2,1,0:T(8,128)(2,1)} %bitcast.21), calls=%async_computation.2 | async-start | bytes 786432 | tf_op jit(solution)/shard_map/all_to_all | solution.py:143
  614.6 7.7 %copy-start.2 = (f32[1,1,3,6,48,256]{5,4,3,2,1,0:T(8,128)S(1)}, f32[1,1,3,6,48,256]{5,4,3,2,1,0:T(8,128)}, u32[]{:S(2)}) copy-start(f32[1,1,3,6,48,256]{5,4,3,2,1,0:T(8,128)} %param.11) | copy-start | bytes 2654212
  (2 other events, 1.9 us)
Sparse Core Ops, SparseCore 0:
  90.4 190.4 all-gather.3
  282.7 146.1 all-gather.5
  431.5 76.6 reduce-scatter.1
  510.6 83.8 all-reduce.2
